TPU v7x, 32 devices: a whole 2x2x4 slice. The times are simulated.
32 devices in a mesh: dp: 4 (over z), cp: 8 (over y, x, core).
Axes of the slice: x: 2, y: 2, z: 4, core: 2. Of those that a mesh axis runs over, the one named last changes fastest.
Arguments:
- row_owner: int32 [4096, 1], P(('dp', 'cp')), may hold values from 0 to 31; in each aligned block of 128 rows (0 to 127, 128 to 255, ...) at most 10 rows name the same one
- slot_row: int32 [4096], P(('dp', 'cp')), may hold values from 0 to 2559
- hot_table: bfloat16 [16384, 512], P(('dp', 'cp')), may hold values from -6 to 6
- cold_table: bfloat16 [65536, 128], P(('dp', 'cp')), may hold values from -6 to 6
- cold_projection: bfloat16 [128, 512], replicated, may hold values from -0.5 to 0.5
- joined_weight: bfloat16 [512, 2048], replicated, may hold values from -0.25 to 0.25
- output_weight: bfloat16 [512, 512], replicated, may hold values from -0.25 to 0.25
- cotangent: bfloat16 [4096, 512], P(('dp', 'cp')), may hold values from -6 to 6
Outputs:
- layer_out: bfloat16 [4096, 512], P(('dp', 'cp'))
- hot_gradient: float32 [16384, 512], P(('dp', 'cp'))
- cold_gradient: float32 [65536, 128], P(('dp', 'cp'))
- projection_gradient: float32 [128, 512], replicated
- joined_gradient: float32 [512, 2048], replicated
- output_gradient: float32 [512, 512], replicated
Inputs may be any that keep to these rules, and one draw needn't show every extreme that they name: `row_owner`: in each aligned block of 128 rows (the rows of one device) no owner is named by more than 10 rows.
All inputs are finite; a program needn't handle non-finite values.
Results may differ from a plain program's by a relative error of at most 0.013.
Values may be sent and summed in bfloat16 or wider, within the bound.
No kernel may reach another device: no remote copies, remote signals or barrier semaphores. Data moves between devices by JAX's collectives and lax.ppermute only.
A program may use at most 128 MiB of HBM per device.

v0:
```python
import math
import jax
import jax.numpy as jnp
from jax import lax
from jax.sharding import PartitionSpec as P

HEADS = 8
EPSILON = 1e-05
block_limit = 1024


def silu_slope(values):
    sigmoid_v = jax.nn.sigmoid(values)
    return sigmoid_v * (1.0 + values * (1.0 - sigmoid_v))


def layer_normalize(values):
    average = jnp.mean(values, axis=-1, keepdims=True)
    centred = values - average
    inverse = lax.rsqrt(jnp.mean(centred * centred, axis=-1, keepdims=True) + EPSILON)
    return (centred * inverse, inverse)


def normalize_back(gradient, normed, inverse):
    first_term = jnp.mean(gradient, axis=-1, keepdims=True)
    second_term = jnp.mean(gradient * normed, axis=-1, keepdims=True)
    return (gradient - first_term - normed * second_term) * inverse


def masked_scores(query_heads, key_heads, query_index, key_index, score_scale):
    scores = (
        jnp.einsum("qhd,khd->hqk", query_heads, key_heads, preferred_element_type=jnp.float32)
        * score_scale
    )
    allowed = (key_index[None, :] <= query_index[:, None])[None]
    weights = jnp.where(allowed, jax.nn.silu(scores), 0.0).astype(jnp.bfloat16)
    return (scores, allowed, weights)


def score_deltas(
    query_heads, key_heads, value_heads, delta_heads, query_index, key_index, score_scale
):
    scores, allowed, weights = masked_scores(
        query_heads, key_heads, query_index, key_index, score_scale
    )
    delta_weights = jnp.einsum(
        "qhd,khd->hqk", delta_heads, value_heads, preferred_element_type=jnp.float32
    )
    delta_scores = jnp.where(allowed, delta_weights * silu_slope(scores) * score_scale, 0.0).astype(
        jnp.bfloat16
    )
    return (weights, delta_scores)


def local(
    row_owner,
    slot_row,
    hot_table,
    cold_table,
    cold_projection,
    joined_weight,
    output_weight,
    cotangent,
):
    tokens_here = slot_row.shape[0]
    model_width = output_weight.shape[0]
    hot_count = hot_table.shape[0]
    cold_count = cold_table.shape[0]
    cold_width = cold_table.shape[1]
    head_count = HEADS
    head_size = model_width // head_count
    score_scale = 1.0 / math.sqrt(head_size)
    devices = lax.axis_size(("dp", "cp"))
    group_index = lax.axis_index("cp")
    capacity = 2 * tokens_here // devices + 2
    owners = row_owner[:, 0]
    is_hot = slot_row < hot_count
    is_cold = jnp.logical_not(is_hot)
    onehot = (owners[:, None] == jnp.arange(devices, dtype=jnp.int32)[None, :]).astype(jnp.bfloat16)
    lower_mask = (jnp.arange(tokens_here)[:, None] > jnp.arange(tokens_here)[None, :]).astype(
        jnp.bfloat16
    )
    earlier = jnp.dot(lower_mask, onehot, preferred_element_type=jnp.float32)
    rank_in_owner = jnp.sum(earlier * onehot.astype(jnp.float32), axis=1).astype(jnp.int32)
    slot_index = owners * capacity + rank_in_owner
    requests = (
        jnp.full((devices * capacity,), -1, jnp.int32)
        .at[slot_index]
        .set(slot_row)
        .reshape(devices, capacity)
    )
    asked_rows = lax.all_to_all(requests, ("dp", "cp"), split_axis=0, concat_axis=0, tiled=True)
    valid_hot = (asked_rows >= 0) & (asked_rows < hot_count)
    valid_cold = asked_rows >= hot_count
    nothing = jnp.zeros((), jnp.bfloat16)
    hot_pick = jnp.where(
        valid_hot[..., None], hot_table[jnp.clip(asked_rows, 0, hot_count - 1)], nothing
    )
    cold_pick = jnp.where(
        valid_cold[..., None],
        cold_table[jnp.clip(asked_rows - hot_count, 0, cold_count - 1)],
        nothing,
    )
    hot_back, cold_back = (
        lax.all_to_all(hot_pick, ("dp", "cp"), split_axis=0, concat_axis=0, tiled=True),
        lax.all_to_all(cold_pick, ("dp", "cp"), split_axis=0, concat_axis=0, tiled=True),
    )
    hot_vector = hot_back.reshape(devices * capacity, model_width)[slot_index]
    cold_vector = cold_back.reshape(devices * capacity, cold_width)[slot_index]
    cold_embed = jnp.dot(cold_vector, cold_projection, preferred_element_type=jnp.float32)
    embedded = jnp.where(is_hot[:, None], hot_vector.astype(jnp.float32), cold_embed)
    normed, inverse = layer_normalize(embedded)
    normed_low = normed.astype(jnp.bfloat16)
    hidden = jnp.dot(normed_low, joined_weight, preferred_element_type=jnp.float32)
    active = jax.nn.silu(hidden).astype(jnp.bfloat16)
    gate_part = active[:, :model_width]
    attention_rows = active[:, model_width:]
    segments = [(0, tokens_here, group_index * tokens_here)]
    value_rows = attention_rows[:, :model_width]
    query_rows = attention_rows[:, model_width : 2 * model_width]
    key_rows = attention_rows[:, 2 * model_width :]
    local_index = jnp.concatenate(
        [first + jnp.arange(count, dtype=jnp.int32) for start, count, first in segments]
    )
    all_keys, all_values = (
        lax.all_gather(key_rows, "cp", axis=0, tiled=True),
        lax.all_gather(value_rows, "cp", axis=0, tiled=True),
    )
    length = all_keys.shape[0]
    key_span = min(length, block_limit)
    heads_shape = (tokens_here, head_count, head_size)
    query_heads = query_rows.reshape(heads_shape)

    def key_slices(counter):
        offset = counter * key_span
        key_block = lax.dynamic_slice_in_dim(all_keys, offset, key_span, 0).reshape(
            key_span, head_count, head_size
        )
        value_block = lax.dynamic_slice_in_dim(all_values, offset, key_span, 0).reshape(
            key_span, head_count, head_size
        )
        key_index = offset + jnp.arange(key_span, dtype=jnp.int32)
        return (offset, key_block, value_block, key_index)

    def blocks_needed(first, count):
        return (first + count + key_span - 1) // key_span

    start, count, first = segments[0]
    segment_queries = query_heads
    segment_index = first + jnp.arange(count, dtype=jnp.int32)

    def forward_step(
        counter, running, segment_queries=segment_queries, segment_index=segment_index
    ):
        offset, key_block, value_block, key_index = key_slices(counter)
        scores, allowed, weights = masked_scores(
            segment_queries, key_block, segment_index, key_index, score_scale
        )
        return running + jnp.einsum(
            "hqk,khd->qhd", weights, value_block, preferred_element_type=jnp.float32
        )

    empty_part = jnp.zeros((count, head_count, head_size), jnp.float32)
    attended_parts = lax.fori_loop(0, blocks_needed(first, count), forward_step, empty_part)
    attended = attended_parts.reshape(tokens_here, model_width)
    mixed, inverse_mix = layer_normalize(attended)
    gated = (mixed * gate_part.astype(jnp.float32)).astype(jnp.bfloat16)
    branch = jnp.dot(gated, output_weight, preferred_element_type=jnp.float32)
    layer_out = (embedded + branch).astype(jnp.bfloat16)
    delta_gated = jnp.dot(cotangent, output_weight.T, preferred_element_type=jnp.float32)
    delta_gate = delta_gated * mixed
    delta_attended = normalize_back(
        delta_gated * gate_part.astype(jnp.float32), mixed, inverse_mix
    ).astype(jnp.bfloat16)
    delta_heads = delta_attended.reshape(heads_shape)
    empty_heads = jnp.zeros(heads_shape, jnp.float32)
    start, count, first = segments[0]
    segment_queries = query_heads
    segment_deltas = delta_heads
    segment_index = first + jnp.arange(count, dtype=jnp.int32)

    def query_step(
        counter,
        running,
        segment_queries=segment_queries,
        segment_deltas=segment_deltas,
        segment_index=segment_index,
    ):
        offset, key_block, value_block, key_index = key_slices(counter)
        weights, delta_scores = score_deltas(
            segment_queries,
            key_block,
            value_block,
            segment_deltas,
            segment_index,
            key_index,
            score_scale,
        )
        return running + jnp.einsum(
            "hqk,khd->qhd", delta_scores, key_block, preferred_element_type=jnp.float32
        )

    empty_part = jnp.zeros((count, head_count, head_size), jnp.float32)
    query_parts = lax.fori_loop(0, blocks_needed(first, count), query_step, empty_part)
    key_heads = key_rows.reshape(heads_shape)
    value_heads = value_rows.reshape(heads_shape)
    key_lowest = jnp.min(local_index)
    query_piece = lax.all_gather(query_rows, "cp", axis=0, tiled=True)
    delta_piece = lax.all_gather(delta_attended, "cp", axis=0, tiled=True)
    row_count = query_piece.shape[0]
    sub_rows = math.gcd(row_count, block_limit)

    def inner_step(counter, partial_sums):
        start_row = counter * sub_rows
        query_block = lax.dynamic_slice_in_dim(query_piece, start_row, sub_rows, 0).reshape(
            sub_rows, head_count, head_size
        )
        delta_block = lax.dynamic_slice_in_dim(delta_piece, start_row, sub_rows, 0).reshape(
            sub_rows, head_count, head_size
        )
        query_index = start_row + jnp.arange(sub_rows, dtype=jnp.int32)

        def accumulate(sums_in):
            weights, delta_scores = score_deltas(
                query_block,
                key_heads,
                value_heads,
                delta_block,
                query_index,
                local_index,
                score_scale,
            )
            key_sum = sums_in[0] + jnp.einsum(
                "hqk,qhd->khd", delta_scores, query_block, preferred_element_type=jnp.float32
            )
            value_sum = sums_in[1] + jnp.einsum(
                "hqk,qhd->khd", weights, delta_block, preferred_element_type=jnp.float32
            )
            return (key_sum, value_sum)

        return lax.cond(
            jnp.max(query_index) >= key_lowest, accumulate, lambda sums_in: sums_in, partial_sums
        )

    key_sum, value_sum = lax.fori_loop(
        0, row_count // sub_rows, inner_step, (empty_heads, empty_heads)
    )
    delta_key = key_sum.reshape(tokens_here, model_width)
    delta_value = value_sum.reshape(tokens_here, model_width)
    attention_grads = jnp.concatenate(
        [delta_value, query_parts.reshape(tokens_here, model_width), delta_key], axis=1
    )
    delta_active = jnp.concatenate([delta_gate, attention_grads], axis=1)
    delta_hidden = (delta_active * silu_slope(hidden)).astype(jnp.bfloat16)
    delta_normed = jnp.dot(delta_hidden, joined_weight.T, preferred_element_type=jnp.float32)
    delta_embed = normalize_back(delta_normed, normed, inverse) + cotangent.astype(jnp.float32)
    cold_float = jnp.where(is_cold[:, None], cold_vector.astype(jnp.float32), 0.0)
    joined_local = jnp.dot(normed_low.T, delta_hidden, preferred_element_type=jnp.float32)
    output_local = jnp.dot(gated.T, cotangent, preferred_element_type=jnp.float32)
    projection_local = jnp.dot(cold_float.T, delta_embed, precision=lax.Precision.HIGHEST)
    joined_sum, output_sum, projection_sum = lax.psum(
        (joined_local, output_local, projection_local), ("dp", "cp")
    )
    norm_scale = (tokens_here * devices) ** (-0.5)
    cold_event = jnp.where(
        is_cold[:, None],
        jnp.dot(
            delta_embed, cold_projection.astype(jnp.float32).T, precision=lax.Precision.HIGHEST
        ),
        0.0,
    )
    hot_event = jnp.where(is_hot[:, None], delta_embed, 0.0)
    hot_buffer = (
        jnp.zeros((devices * capacity, model_width), jnp.float32)
        .at[slot_index]
        .set(hot_event)
        .reshape(devices, capacity, model_width)
    )
    cold_buffer = (
        jnp.zeros((devices * capacity, cold_width), jnp.float32)
        .at[slot_index]
        .set(cold_event)
        .reshape(devices, capacity, cold_width)
    )
    hot_arrived, cold_arrived = (
        lax.all_to_all(hot_buffer, ("dp", "cp"), split_axis=0, concat_axis=0, tiled=True),
        lax.all_to_all(cold_buffer, ("dp", "cp"), split_axis=0, concat_axis=0, tiled=True),
    )
    hot_target = jnp.where(valid_hot, asked_rows, hot_count).reshape(-1)
    cold_target = jnp.where(valid_cold, asked_rows - hot_count, cold_count).reshape(-1)
    hot_gradient = (
        jnp.zeros((hot_count, model_width), jnp.float32)
        .at[hot_target]
        .add(hot_arrived.reshape(-1, model_width), mode="drop")
    )
    cold_gradient = (
        jnp.zeros((cold_count, cold_width), jnp.float32)
        .at[cold_target]
        .add(cold_arrived.reshape(-1, cold_width), mode="drop")
    )
    return (
        layer_out,
        hot_gradient,
        cold_gradient,
        projection_sum * norm_scale,
        joined_sum * norm_scale,
        output_sum * norm_scale,
    )


def solution(mesh):
    placed = (
        P(("dp", "cp"), None),
        P(("dp", "cp")),
        P(("dp", "cp"), None),
        P(("dp", "cp"), None),
        P(),
        P(),
        P(),
        P(("dp", "cp"), None),
    )
    return jax.shard_map(
        local,
        mesh=mesh,
        in_specs=placed,
        out_specs=(
            P(("dp", "cp"), None),
            P(("dp", "cp"), None),
            P(("dp", "cp"), None),
            P(),
            P(),
            P(),
        ),
        check_vma=False,
    )
```

profile of v0, /device:TPU:0, one launch (start us, length us, event | category | flops | bytes accessed | tf_op | source)
XLA Modules:
  0.0 384.5 jit_solution(10527699452270542202)
XLA Ops:
  7.2 1.0 fusion.29
  8.9 1.1 scatter_custom_fusion
  10.7 7.3 %all-to-all-start = ((s32[32,1,10]{2,1,0:T(1,128)}), s32[32,1,10]{2,1,0:T(1,128)S(1)}, u32[]{:S(2)}, u32[]{:S(2)}) async-start(s32[32,1,10]{2,1,0:T(1,128)} %bitcast.9), calls=%async_computation | async-start | bytes 32768 | tf_op jit(solution)/shard_map/all_to_all | solution.py:92
  18.0 7.1 %all-to-all-done = s32[32,1,10]{2,1,0:T(1,128)S(1)} async-done(((s32[32,1,10]{2,1,0:T(1,128)}), s32[32,1,10]{2,1,0:T(1,128)S(1)}, u32[]{:S(2)}, u32[]{:S(2)}) %all-to-all-start) | async-done | bytes 1312 | tf_op jit(solution)/shard_map/all_to_all | solution.py:92
  26.5 2.2 gather_fusion.2
  28.8 0.8 broadcast_select_fusion.1
  29.6 2.6 all-to-all-start.2
  32.3 2.0 gather_fusion
  34.5 0.9 broadcast_select_fusion
  35.4 5.0 %all-to-all-done.2 = bf16[32,10,128]{2,1,0:T(8,128)(2,1)S(1)} async-done(((bf16[32,10,128]{2,1,0:T(8,128)(2,1)}), bf16[32,10,128]{2,1,0:T(8,128)(2,1)S(1)}, u32[]{:S(2)}, u32[]{:S(2)}) %all-to-all-start.2) | async-done | bytes 81952 | tf_op jit(solution)/shard_map/all_to_all | solution.py:106
  40.4 2.6 all-to-all-start.1
  44.4 14.2 %all-to-all-done.1 = bf16[32,10,512]{2,1,0:T(8,128)(2,1)S(1)} async-done(((bf16[32,10,512]{2,1,0:T(8,128)(2,1)}), bf16[32,10,512]{2,1,0:T(8,128)(2,1)S(1)}, u32[]{:S(2)}, u32[]{:S(2)}) %all-to-all-start.1) | async-done | bytes 327712 | tf_op jit(solution)/shard_map/all_to_all | solution.py:105
  58.7 0.8 gather_fusion.1
  60.1 1.5 multiply_convert_fusion
  61.6 0.8 copy-done.7
  66.6 18.3 %all-gather.5.cloned.1.call-done = bf16[1024,512]{1,0:T(8,128)(2,1)} async-done(((bf16[128,512]{1,0:T(8,128)(2,1)}), bf16[1024,512]{1,0:T(8,128)(2,1)}) %all-gather.5.cloned.1.call-update) | async-done | bytes 1048592 | tf_op jit(solution)/shard_map/all_gather | solution.py:126
  84.9 2.3 copy.48
  87.2 23.6 %all-gather.7.cloned.1.call-done = bf16[1024,512]{1,0:T(8,128)(2,1)} async-done(((bf16[128,512]{1,0:T(8,128)(2,1)}), bf16[1024,512]{1,0:T(8,128)(2,1)}) %all-gather.7.cloned.1.call-update) | async-done | bytes 1048592 | tf_op jit(solution)/shard_map/all_gather | solution.py:127
  110.8 1.5 copy.49
  113.0 4.2 %while.28 = (s32[]{:T(128)}, f32[128,8,64]{0,2,1:T(8,128)}, s32[]{:T(128)}, bf16[1024,512]{0,1:T(8,128)(2,1)}, bf16[128,8,64]{0,2,1:T(8,128)(2,1)}, /*index=5*/b...) while((s32[]{:T(128)}, f32[128,8,64]{0,2,1:T(8,128)}, s32[]{:T(128)}, ...), condition=%wide.region_5.6_spmd.clone, body=%wide.region_4.5_spmd.clone.sunk | while | flops 275973248 | bytes 3023985 | solution.py:164
  113.2 4.0 %fusion.115 = f32[128,8,64]{0,2,1:T(8,128)} fusion(f32[128,8,64]{0,2,1:T(8,128)} %get-tuple-element.430, bf16[1024,8,64]{0,2,1:T(8,128)(2,1)S(1)} %bitcast.111, bf16[128,8,64]{0,2,1:T(8,128)(2,1)} %get-tuple-element.442, bf16[1024,8,64]{0,2,1:T(8,128)(2,1)} %bitcast.117, pred[128,1024]{1,0:T(8,128)(4,1)S(1)} %broadcast_compare_fusion.6), kind=kOutput, calls=%fused_computation.30.clone.1 | convolution fusion | flops 275841024 | bytes 2883584 | tf_op jit(solution)/shard_map/while/body/hqk,khd->qhd/dot_general | solution.py:159
  117.2 1.0 reduce_sum.84
  118.2 1.8 copy.50
  120.0 1.0 multiply_reduce_fusion.2
  121.1 1.6 fusion.45
  122.7 2.0 multiply_convert_fusion.1
  124.7 1.0 copy.55
  126.5 9.7 %while.29 = (s32[]{:T(128)}, f32[128,8,64]{0,2,1:T(8,128)}, s32[]{:T(128)}, bf16[1024,512]{0,1:T(8,128)(2,1)S(1)}, bf16[128,8,64]{0,2,1:T(8,128)(2,1)S(1)}, /*in...) while((s32[]{:T(128)}, f32[128,8,64]{0,2,1:T(8,128)}, ...), condition=%wide.region_14.15_spmd.clone, body=%wide.region_13.14_spmd.clone.sunk | while | flops 415433856 | bytes 11543673 | solution.py:204
  126.5 2.8 fusion.121
  129.2 0.8 broadcast_compare_fusion.7
  130.0 6.2 %fusion.122 = f32[128,8,64]{0,2,1:T(8,128)} fusion(f32[128,8,64]{0,2,1:T(8,128)} %get-tuple-element.462, bf16[1024,8,64]{0,2,1:T(8,128)(2,1)} %bitcast.118, f32[8,128,1024]{2,1,0:T(8,128)} %fusion.121, bf16[128,8,64]{0,2,1:T(8,128)(2,1)} %get-tuple-element.477, pred[128,1024]{1,0:T(8,128)(4,1)} %broadcast_compare_fusion.7), kind=kOutput, calls=%fused_computation.40.clone.1 | convolution fusion | flops 281083904 | bytes 6029312 | tf_op jit(solution)/shard_map/while/body/hqk,khd->qhd/dot_general | solution.py:199
  136.2 1.8 copy.59
  138.0 2.2 fusion.71
  140.3 21.0 %all-gather.9.cloned.1.call-done = bf16[1024,512]{1,0:T(8,128)(2,1)} async-done(((bf16[128,512]{1,0:T(8,128)(2,1)}), bf16[1024,512]{1,0:T(8,128)(2,1)}) %all-gather.9.cloned.1.call-update) | async-done | bytes 1048592 | tf_op jit(solution)/shard_map/all_gather | solution.py:209
  162.6 22.0 %conditional.1 = (f32[128,8,64]{0,2,1:T(8,128)}, f32[128,8,64]{0,2,1:T(8,128)}) conditional(s32[]{:T(128)} %convert_element_type.78, f32[128,8,64]{0,2,1:T(8,128)} %broadcast.362, (s32[128]{0:T(128)}, s32[1024]{0:T(1024)}, bf16[1024,512]{1,0:T(8,128)(2,1)}, bf16[128,512]{1,0:T(8,128)(2,1)}, bf16[1024,512]{1,0:T(8,128)(2,1)}, ...), branch_computations={%region_11.12_spmd, %region_12.13_spmd} | conditional | flops 557056000 | bytes 24253000 | solution.py:241
  162.6 1.5 copy.53
  164.1 1.7 copy.54
  165.8 3.7 fusion.69
  169.5 2.3 copy.51
  171.8 1.5 broadcast_compare_fusion
  173.3 0.8 copy.52
  174.1 5.9 %fusion.9 = f32[128,8,64]{0,2,1:T(8,128)} fusion(f32[128,8,64]{0,2,1:T(8,128)} %get-tuple-element.132, bf16[1024,8,64]{0,2,1:T(8,128)(2,1)S(1)} %bitcast.116, f32[8,1024,128]{2,1,0:T(8,128)} %fusion.69, bf16[1024,8,64]{0,2,1:T(8,128)(2,1)} %bitcast.119, bf16[128,8,64]{0,2,1:T(8,128)(2,1)} %bitcast.126, pred[1024,128]{1,0:T(8,128)(4,1)} %broadcast_compare_fusion), kind=kOutput, calls=%fused_computation.19 | convolution fusion | flops 281083904 | bytes 7077888 | tf_op jit(solution)/shard_map/while/body/eval_jaxpr/cond/branch_1_fun/hqk,qhd->khd/dot_general | solution.py:233
  180.0 4.6 %fusion.8 = f32[128,8,64]{0,2,1:T(8,128)} fusion(f32[128,8,64]{0,2,1:T(8,128)} %get-tuple-element.132, bf16[1024,8,64]{0,2,1:T(8,128)(2,1)} %bitcast.120, f32[8,1024,128]{2,1,0:T(8,128)} %fusion.69, pred[1024,128]{1,0:T(8,128)(4,1)S(1)} %copy-done.13), kind=kOutput, calls=%fused_computation.18 | convolution fusion | flops 141623296 | bytes 5898240 | tf_op jit(solution)/shard_map/while/body/eval_jaxpr/cond/branch_1_fun/hqk,qhd->khd/dot_general | solution.py:236
  184.6 1.1 copy.58
  185.7 1.1 copy.60
  186.8 1.8 fusion.30
  188.5 3.6 fusion.61
  192.1 0.9 fusion.65
  193.3 1.2 fusion.46
  194.8 1.0 scatter_custom_fusion.3
  196.6 4.7 %all-to-all-start.4 = ((f32[32,10,128]{2,1,0:T(8,128)}), f32[32,10,128]{2,1,0:T(8,128)}, u32[]{:S(2)}, u32[]{:S(2)}) async-start(f32[32,10,128]{2,1,0:T(8,128)} %reshape.392), calls=%async_computation.4 | async-start | bytes 524288 | tf_op jit(solution)/shard_map/all_to_all | solution.py:287
  201.3 1.4 scatter_custom_fusion.1
  202.7 1.1 reshape.390
  203.7 11.2 %all-to-all-done.4 = f32[32,10,128]{2,1,0:T(8,128)} async-done(((f32[32,10,128]{2,1,0:T(8,128)}), f32[32,10,128]{2,1,0:T(8,128)}, u32[]{:S(2)}, u32[]{:S(2)}) %all-to-all-start.4) | async-done | bytes 163872 | tf_op jit(solution)/shard_map/all_to_all | solution.py:287
  214.9 2.7 all-to-all-start.3
  219.0 2.0 fusion.28
  220.9 1.0 reshape.462
  221.9 2.6 scatter_custom_fusion.4
  224.5 30.8 %all-to-all-done.3 = f32[32,10,512]{2,1,0:T(8,128)S(1)} async-done(((f32[32,10,512]{2,1,0:T(8,128)}), f32[32,10,512]{2,1,0:T(8,128)S(1)}, u32[]{:S(2)}, u32[]{:S(2)}) %all-to-all-start.3) | async-done | bytes 655392 | tf_op jit(solution)/shard_map/all_to_all | solution.py:286
  255.3 0.9 reshape.446
  256.2 4.0 %scatter_custom_fusion.2 = f32[512,512]{1,0:T(8,128)} fusion(s32[320]{0:T(512)S(1)} %get-tuple-element.272, f32[320,512]{1,0:T(8,128)} %reshape.446, f32[]{:T(128)} %constant.57.clone.1), kind=kCustom, calls=%fused_computation.61 | custom fusion | flops 163840 | bytes 1049088 | tf_op jit(solution)/shard_map/scatter-add | solution.py:294
  260.2 111.1 %all-reduce.3.cloned.1.call-done = (f32[128,512]{1,0:T(8,128)}, f32[512,2048]{1,0:T(8,128)}, f32[512,512]{1,0:T(8,128)}) async-done(((f32[128,512]{1,0:T(8,128)}, f32[512,2048]{1,0:T(8,128)}, f32[512,512]{1,0:T(8,128)}), (f32[128,512]{1,0:T(8,128)}, f32[512,2048]{1,0:T(8,128)}, f32[512,512]{1,0:T(8,128)})) %all-reduce.3.cloned.1.call-update) | async-done | bytes 5505040 | tf_op jit(solution)/shard_map/psum | solution.py:261
  371.3 4.9 %broadcast_multiply_fusion = f32[512,2048]{1,0:T(8,128)} fusion(f32[512,2048]{1,0:T(8,128)} %get-tuple-element.304), kind=kLoop, calls=%fused_computation.47 | loop fusion | flops 1048576 | bytes 8388608 | tf_op jit(solution)/shard_map/mul | solution.py:306
  376.2 1.1 broadcast_multiply_fusion.1
  (103 shorter events, 14.8 us)
Async XLA Ops:
  7.2 52.9 %copy-start = (bf16[512,2048]{1,0:T(8,128)(2,1)S(1)}, bf16[512,2048]{1,0:T(8,128)(2,1)}, u32[]{:S(2)}) copy-start(bf16[512,2048]{1,0:T(8,128)(2,1)} %param.19) | copy-start | bytes 6291460
  7.2 25.1 %copy-start.1 = (bf16[512,512]{1,0:T(8,128)(2,1)S(1)}, bf16[512,512]{1,0:T(8,128)(2,1)}, u32[]{:S(2)}) copy-start(bf16[512,512]{1,0:T(8,128)(2,1)} %param.16) | copy-start | bytes 1572868
  8.9 34.2 %copy-start.21 = (s32[128]{0:T(128)}, s32[128]{0:T(128)S(1)}, u32[]{:S(2)}) copy-start(s32[128]{0:T(128)S(1)} %fusion.57) | copy-start | bytes 1540
  10.7 14.4 %all-to-all-start = ((s32[32,1,10]{2,1,0:T(1,128)}), s32[32,1,10]{2,1,0:T(1,128)S(1)}, u32[]{:S(2)}, u32[]{:S(2)}) async-start(s32[32,1,10]{2,1,0:T(1,128)} %bitcast.9), calls=%async_computation | async-start | bytes 32768 | tf_op jit(solution)/shard_map/all_to_all | solution.py:92
  28.8 14.3 %copy-start.22 = (s32[128]{0:T(128)S(1)}, s32[128]{0:T(128)}, u32[]{:S(2)}) copy-start(s32[128]{0:T(128)} %param.15) | copy-start | bytes 1540
  29.6 10.8 %all-to-all-start.2 = ((bf16[32,10,128]{2,1,0:T(8,128)(2,1)}), bf16[32,10,128]{2,1,0:T(8,128)(2,1)S(1)}, u32[]{:S(2)}, u32[]{:S(2)}) async-start(bf16[32,10,128]{2,1,0:T(8,128)(2,1)} %broadcast_select_fusion.1), calls=%async_computation.2 | async-start | bytes 262144 | tf_op jit(solution)/shard_map/all_to_all | solution.py:106
  32.3 27.3 %copy-start.8 = (bf16[128,512]{1,0:T(8,128)(2,1)S(1)}, bf16[128,512]{1,0:T(8,128)(2,1)}, u32[]{:S(2)}) copy-start(bf16[128,512]{1,0:T(8,128)(2,1)} %param.18) | copy-start | bytes 393220
  40.4 18.2 %all-to-all-start.1 = ((bf16[32,10,512]{2,1,0:T(8,128)(2,1)}), bf16[32,10,512]{2,1,0:T(8,128)(2,1)S(1)}, u32[]{:S(2)}, u32[]{:S(2)}) async-start(bf16[32,10,512]{2,1,0:T(8,128)(2,1)} %broadcast_select_fusion), calls=%async_computation.1 | async-start | bytes 1048576 | tf_op jit(solution)/shard_map/all_to_all | solution.py:105
  43.0 41.9 %all-gather.5.cloned.1.call-start = ((), (), s32[]{:S(2)}) async-start(), calls=%async_computation.5 | async-start | bytes 1179648 | tf_op jit(solution)/shard_map/all_gather | solution.py:126
  43.7 16.2 %copy-start.18 = (pred[128]{0:T(512)(128)(4,1)}, pred[128]{0:T(512)(128)(4,1)S(1)}, u32[]{:S(2)}) copy-start(pred[128]{0:T(512)(128)(4,1)S(1)} %get-tuple-element.317) | copy-start | bytes 388
  44.4 17.2 %copy-start.10 = (bf16[128,128]{1,0:T(8,128)(2,1)}, bf16[128,128]{1,0:T(8,128)(2,1)S(1)}, u32[]{:S(2)}) copy-start(bf16[128,128]{1,0:T(8,128)(2,1)S(1)} %gather_fusion.3) | copy-start | bytes 98308
  59.9 27.3 %copy-start.14 = (f32[128]{0:T(128)}, f32[128]{0:T(128)S(1)}, u32[]{:S(2)}) copy-start(f32[128]{0:T(128)S(1)} %broadcast_multiply_fusion.8) | copy-start | bytes 1540
  60.1 27.1 %copy-start.16 = (f32[128]{0:T(128)}, f32[128]{0:T(128)S(1)}, u32[]{:S(2)}) copy-start(f32[128]{0:T(128)S(1)} %add_rsqrt_fusion.1) | copy-start | bytes 1540
  61.6 0.8 copy-start.7
  63.1 3.4 copy-start.4
  63.1 47.7 %all-gather.7.cloned.1.call-start = ((), (), s32[]{:S(2)}) async-start(), calls=%async_computation.6 | async-start | bytes 1179648 | tf_op jit(solution)/shard_map/all_gather | solution.py:127
  63.9 76.4 %all-gather.11.cloned.1.call-start = ((), (), s32[]{:S(2)}) async-start(), calls=%async_computation.8 | async-start | bytes 1179648 | tf_op jit(solution)/shard_map/all_gather | solution.py:208
  66.5 94.7 %all-gather.9.cloned.1.call-start = ((), (), s32[]{:S(2)}) async-start(), calls=%async_computation.7 | async-start | bytes 1179648 | tf_op jit(solution)/shard_map/all_gather | solution.py:209
  125.7 245.6 %all-reduce.3.cloned.1.call-start = ((), (), s32[]{:S(2)}) async-start(), calls=%async_computation.9 | async-start | bytes 11010048 | tf_op jit(solution)/shard_map/psum | solution.py:261
  164.1 9.2 %copy-start.3 = (bf16[128,512]{1,0:T(8,128)(2,1)S(1)}, bf16[128,512]{1,0:T(8,128)(2,1)}, u32[]{:S(2)}) copy-start(bf16[128,512]{1,0:T(8,128)(2,1)} %get-tuple-element.255) | copy-start | bytes 393220 | tf_op jit(solution)/shard_map/while/body/eval_jaxpr/cond
  174.1 5.9 %copy-start.13 = (pred[1024,128]{1,0:T(8,128)(4,1)S(1)}, pred[1024,128]{1,0:T(8,128)(4,1)}, u32[]{:S(2)}) copy-start(pred[1024,128]{1,0:T(8,128)(4,1)} %broadcast_compare_fusion) | copy-start | bytes 393220 | tf_op jit(solution)/shard_map/while/body/eval_jaxpr/cond
  185.6 6.5 %copy-start.15 = (f32[128]{0:T(128)S(1)}, f32[128]{0:T(128)}, u32[]{:S(2)}) copy-start(f32[128]{0:T(128)} %copy-done.14) | copy-start | bytes 1540
  185.7 6.4 %copy-start.17 = (f32[128]{0:T(128)S(1)}, f32[128]{0:T(128)}, u32[]{:S(2)}) copy-start(f32[128]{0:T(128)} %copy-done.16) | copy-start | bytes 1540
  188.5 4.5 %copy-start.2 = (bf16[128,512]{1,0:T(8,128)(2,1)S(1)}, bf16[128,512]{1,0:T(8,128)(2,1)}, u32[]{:S(2)}) copy-start(bf16[128,512]{1,0:T(8,128)(2,1)} %param.21) | copy-start | bytes 393220
  188.5 4.7 %copy-start.11 = (bf16[128,128]{1,0:T(8,128)(2,1)S(1)}, bf16[128,128]{1,0:T(8,128)(2,1)}, u32[]{:S(2)}) copy-start(bf16[128,128]{1,0:T(8,128)(2,1)} %copy-done.10) | copy-start | bytes 98308
  188.5 4.7 %copy-start.20 = (pred[128]{0:T(512)(128)(4,1)S(1)}, pred[128]{0:T(512)(128)(4,1)}, u32[]{:S(2)}) copy-start(pred[128]{0:T(512)(128)(4,1)} %get-tuple-element.316) | copy-start | bytes 388
  193.0 1.5 copy-start.9
  193.1 8.2 %copy-start.19 = (pred[128]{0:T(512)(128)(4,1)S(1)}, pred[128]{0:T(512)(128)(4,1)}, u32[]{:S(2)}) copy-start(pred[128]{0:T(512)(128)(4,1)} %copy-done.18) | copy-start | bytes 388
  194.5 24.5 %copy-start.5 = (bf16[128,512]{1,0:T(8,128)(2,1)S(1)}, bf16[128,512]{1,0:T(8,128)(2,1)}, u32[]{:S(2)}) copy-start(bf16[128,512]{1,0:T(8,128)(2,1)} %get-tuple-element.307) | copy-start | bytes 393220
  196.6 18.4 %all-to-all-start.4 = ((f32[32,10,128]{2,1,0:T(8,128)}), f32[32,10,128]{2,1,0:T(8,128)}, u32[]{:S(2)}, u32[]{:S(2)}) async-start(f32[32,10,128]{2,1,0:T(8,128)} %reshape.392), calls=%async_computation.4 | async-start | bytes 524288 | tf_op jit(solution)/shard_map/all_to_all | solution.py:287
  214.9 40.4 %all-to-all-start.3 = ((f32[32,10,512]{2,1,0:T(8,128)}), f32[32,10,512]{2,1,0:T(8,128)S(1)}, u32[]{:S(2)}, u32[]{:S(2)}) async-start(f32[32,10,512]{2,1,0:T(8,128)} %reshape.390), calls=%async_computation.3 | async-start | bytes 2097152 | tf_op jit(solution)/shard_map/all_to_all | solution.py:286
  371.3 4.9 %copy-start.6 = (f32[512,512]{1,0:T(8,128)S(1)}, f32[512,512]{1,0:T(8,128)}, u32[]{:S(2)}) copy-start(f32[512,512]{1,0:T(8,128)} %get-tuple-element.305) | copy-start | bytes 3145732
  371.3 6.0 %copy-start.12 = (f32[128,512]{1,0:T(8,128)S(1)}, f32[128,512]{1,0:T(8,128)}, u32[]{:S(2)}) copy-start(f32[128,512]{1,0:T(8,128)} %get-tuple-element.303) | copy-start | bytes 786436
Sparse Core Ops, SparseCore 0:
  63.3 21.6 all-gather.4
  87.4 23.3 all-gather.6
  112.7 23.3 all-gather.10
  137.9 23.3 all-gather.8
  194.6 176.6 all-reduce.2
where the time goes:
time: 386 us; the launch traced here: 385 us
  waiting for transfers between devices  243 us (63%)
  matrix products  41.7 us (11%)
  local copies, waits for them, and re-layouts  35.9 us (9%)
  other arithmetic  28.9 us (7%)
  starting transfers between devices  20.1 us (5%)
  between operations  14.9 us (4%)
    psum x1, waiting for transfers between devices, local(): lax.psum((joined_local, output_local, projection_local), ('dp', 'cp'))  111 us
    all_to_all x1, waiting for transfers between devices, local(): lax.all_to_all(hot_buffer, ('dp', 'cp'), split_axis=0, concat_axis=0, til...  30.8 us
    all_gather x1, waiting for transfers between devices, local(): lax.all_gather(value_rows, 'cp', axis=0, tiled=True)  23.6 us
    all_gather x1, waiting for transfers between devices, local(): delta_piece = lax.all_gather(delta_attended, 'cp', axis=0, tiled=True)  21 us
    all_gather x1, waiting for transfers between devices, local(): lax.all_gather(key_rows, 'cp', axis=0, tiled=True)  18.3 us
    all_to_all x1, waiting for transfers between devices, local(): lax.all_to_all(hot_pick, ('dp', 'cp'), split_axis=0, concat_axis=0, tiled...  14.2 us
    all_to_all x1, waiting for transfers between devices, local(): lax.all_to_all(cold_buffer, ('dp', 'cp'), split_axis=0, concat_axis=0, ti...  11.2 us
    another operation x8, local copies, waits for them, and re-layouts  8.38 us
  transfers between devices with their start and end apart: 10, of which 9 were waited for; matrix products, arithmetic and copies ran while one was open for 14% of the time, Pallas kernels for 0%

commit v1 on v0

--- a/solution.py
+++ b/solution.py
@@ -259,7 +259,7 @@
     output_local = jnp.dot(gated.T, cotangent, preferred_element_type=jnp.float32)
     projection_local = jnp.dot(cold_float.T, delta_embed, precision=lax.Precision.HIGHEST)
     joined_sum, output_sum, projection_sum = lax.psum(
-        (joined_local, output_local, projection_local), ("dp", "cp")
+        lax.psum((joined_local, output_local, projection_local), "cp"), "dp"
     )
     norm_scale = (tokens_here * devices) ** (-0.5)
     cold_event = jnp.where(

time: 386 us -> 532 us (1.38)
  waiting for transfers between devices: 243 us -> 385 us
    psum x1 -> x2, waiting for transfers between devices: 111 us -> 235 us  [the longest x1 140 us: local(): lax.psum(lax.psum((joined_local, output_local, projection_local), 'cp'),...]
    all_to_all x1, waiting for transfers between devices: 30.8 us -> 45.8 us  [local(): lax.all_to_all(hot_buffer, ('dp', 'cp'), split_axis=0, concat_axis=0, til...]
  transfers between devices with their start and end apart: 10 -> 11, of which waited for: 9 -> 10; matrix products, arithmetic and copies ran while one was open for 14% -> 10% of each run, Pallas kernels for 0% -> 0%
where the time goes in v1:
time: 532 us; the launch traced here: 531 us
  waiting for transfers between devices  385 us (72%)
  matrix products  41.7 us (8%)
  local copies, waits for them, and re-layouts  35.8 us (7%)
  other arithmetic  28.9 us (5%)
  starting transfers between devices  24.6 us (5%)
  between operations  15.3 us (3%)
    psum x1, waiting for transfers between devices, local(): lax.psum(lax.psum((joined_local, output_local, projection_local), 'cp'),...  140 us
    psum x1, waiting for transfers between devices, local(): lax.psum((joined_local, output_local, projection_local), 'cp')  95.4 us
    all_to_all x1, waiting for transfers between devices, local(): lax.all_to_all(hot_buffer, ('dp', 'cp'), split_axis=0, concat_axis=0, til...  45.8 us
    all_gather x1, waiting for transfers between devices, local(): lax.all_gather(value_rows, 'cp', axis=0, tiled=True)  23.6 us
    all_gather x1, waiting for transfers between devices, local(): delta_piece = lax.all_gather(delta_attended, 'cp', axis=0, tiled=True)  21 us
    all_gather x1, waiting for transfers between devices, local(): lax.all_gather(key_rows, 'cp', axis=0, tiled=True)  18.4 us
    all_to_all x1, waiting for transfers between devices, local(): lax.all_to_all(hot_pick, ('dp', 'cp'), split_axis=0, concat_axis=0, tiled...  14.2 us
    all_to_all x1, waiting for transfers between devices, local(): lax.all_to_all(cold_buffer, ('dp', 'cp'), split_axis=0, concat_axis=0, ti...  13.7 us
  transfers between devices with their start and end apart: 11, of which 10 were waited for; matrix products, arithmetic and copies ran while one was open for 10% of the time, Pallas kernels for 0%

profile of v1, /device:TPU:0, one launch (start us, length us, event | category | flops | bytes accessed | tf_op | source)
XLA Modules:
  0.0 530.9 jit_solution(9245627003133395092)
XLA Ops:
  7.2 1.0 fusion.29
  8.9 1.1 scatter_custom_fusion
  10.7 7.3 %all-to-all-start = ((s32[32,1,10]{2,1,0:T(1,128)}), s32[32,1,10]{2,1,0:T(1,128)S(1)}, u32[]{:S(2)}, u32[]{:S(2)}) async-start(s32[32,1,10]{2,1,0:T(1,128)} %bitcast.9), calls=%async_computation | async-start | bytes 32768 | tf_op jit(solution)/shard_map/all_to_all | solution.py:92
  18.0 7.1 %all-to-all-done = s32[32,1,10]{2,1,0:T(1,128)S(1)} async-done(((s32[32,1,10]{2,1,0:T(1,128)}), s32[32,1,10]{2,1,0:T(1,128)S(1)}, u32[]{:S(2)}, u32[]{:S(2)}) %all-to-all-start) | async-done | bytes 1312 | tf_op jit(solution)/shard_map/all_to_all | solution.py:92
  26.5 2.2 gather_fusion.2
  28.8 0.8 broadcast_select_fusion.1
  29.6 2.6 all-to-all-start.2
  32.3 2.0 gather_fusion
  34.5 0.9 broadcast_select_fusion
  35.4 5.0 all-to-all-done.2
  40.4 2.6 all-to-all-start.1
  44.4 14.2 %all-to-all-done.1 = bf16[32,10,512]{2,1,0:T(8,128)(2,1)S(1)} async-done(((bf16[32,10,512]{2,1,0:T(8,128)(2,1)}), bf16[32,10,512]{2,1,0:T(8,128)(2,1)S(1)}, u32[]{:S(2)}, u32[]{:S(2)}) %all-to-all-start.1) | async-done | bytes 327712 | tf_op jit(solution)/shard_map/all_to_all | solution.py:105
  58.7 0.8 gather_fusion.1
  60.1 1.5 multiply_convert_fusion
  61.6 0.8 copy-done.7
  66.6 18.4 %all-gather.5.cloned.1.call-done = bf16[1024,512]{1,0:T(8,128)(2,1)} async-done(((bf16[128,512]{1,0:T(8,128)(2,1)}), bf16[1024,512]{1,0:T(8,128)(2,1)}) %all-gather.5.cloned.1.call-update) | async-done | bytes 1048592 | tf_op jit(solution)/shard_map/all_gather | solution.py:126
  85.0 2.3 copy.48
  87.2 23.6 %all-gather.7.cloned.1.call-done = bf16[1024,512]{1,0:T(8,128)(2,1)} async-done(((bf16[128,512]{1,0:T(8,128)(2,1)}), bf16[1024,512]{1,0:T(8,128)(2,1)}) %all-gather.7.cloned.1.call-update) | async-done | bytes 1048592 | tf_op jit(solution)/shard_map/all_gather | solution.py:127
  110.8 1.5 copy.49
  113.0 4.2 while.28
  113.2 4.0 fusion.115
  117.2 1.0 reduce_sum.84
  118.3 1.8 copy.50
  120.0 1.0 multiply_reduce_fusion.2
  121.1 1.6 fusion.45
  122.7 1.9 multiply_convert_fusion.1
  124.6 1.0 copy.55
  126.5 9.7 %while.29 = (s32[]{:T(128)}, f32[128,8,64]{0,2,1:T(8,128)}, s32[]{:T(128)}, bf16[1024,512]{0,1:T(8,128)(2,1)S(1)}, bf16[128,8,64]{0,2,1:T(8,128)(2,1)S(1)}, /*in...) while((s32[]{:T(128)}, f32[128,8,64]{0,2,1:T(8,128)}, ...), condition=%wide.region_14.15_spmd.clone, body=%wide.region_13.14_spmd.clone.sunk | while | flops 415433856 | bytes 11543673 | solution.py:204
  126.5 2.8 fusion.121
  129.2 0.8 broadcast_compare_fusion.7
  130.0 6.2 %fusion.122 = f32[128,8,64]{0,2,1:T(8,128)} fusion(f32[128,8,64]{0,2,1:T(8,128)} %get-tuple-element.465, bf16[1024,8,64]{0,2,1:T(8,128)(2,1)} %bitcast.118, f32[8,128,1024]{2,1,0:T(8,128)} %fusion.121, bf16[128,8,64]{0,2,1:T(8,128)(2,1)} %get-tuple-element.480, pred[128,1024]{1,0:T(8,128)(4,1)} %broadcast_compare_fusion.7), kind=kOutput, calls=%fused_computation.40.clone.1 | convolution fusion | flops 281083904 | bytes 6029312 | tf_op jit(solution)/shard_map/while/body/hqk,khd->qhd/dot_general | solution.py:199
  136.2 1.8 copy.59
  138.0 2.3 fusion.71
  140.2 21.0 %all-gather.9.cloned.1.call-done = bf16[1024,512]{1,0:T(8,128)(2,1)} async-done(((bf16[128,512]{1,0:T(8,128)(2,1)}), bf16[1024,512]{1,0:T(8,128)(2,1)}) %all-gather.9.cloned.1.call-update) | async-done | bytes 1048592 | tf_op jit(solution)/shard_map/all_gather | solution.py:209
  162.6 22.0 %conditional.1 = (f32[128,8,64]{0,2,1:T(8,128)}, f32[128,8,64]{0,2,1:T(8,128)}) conditional(s32[]{:T(128)} %convert_element_type.78, f32[128,8,64]{0,2,1:T(8,128)} %broadcast.362, (s32[128]{0:T(128)}, s32[1024]{0:T(1024)}, bf16[1024,512]{1,0:T(8,128)(2,1)}, bf16[128,512]{1,0:T(8,128)(2,1)}, bf16[1024,512]{1,0:T(8,128)(2,1)}, ...), branch_computations={%region_11.12_spmd, %region_12.13_spmd} | conditional | flops 557056000 | bytes 24253000 | solution.py:241
  162.6 1.5 copy.53
  164.1 1.7 copy.54
  165.8 3.7 fusion.69
  169.5 2.3 copy.51
  171.8 1.5 broadcast_compare_fusion
  174.1 5.9 %fusion.9 = f32[128,8,64]{0,2,1:T(8,128)} fusion(f32[128,8,64]{0,2,1:T(8,128)} %get-tuple-element.132, bf16[1024,8,64]{0,2,1:T(8,128)(2,1)S(1)} %bitcast.116, f32[8,1024,128]{2,1,0:T(8,128)} %fusion.69, bf16[1024,8,64]{0,2,1:T(8,128)(2,1)} %bitcast.119, bf16[128,8,64]{0,2,1:T(8,128)(2,1)} %bitcast.126, pred[1024,128]{1,0:T(8,128)(4,1)} %broadcast_compare_fusion), kind=kOutput, calls=%fused_computation.19 | convolution fusion | flops 281083904 | bytes 7077888 | tf_op jit(solution)/shard_map/while/body/eval_jaxpr/cond/branch_1_fun/hqk,qhd->khd/dot_general | solution.py:233
  180.0 4.6 fusion.8
  184.6 1.1 copy.58
  185.7 1.1 copy.60
  186.8 1.8 fusion.30
  188.6 3.6 fusion.61
  192.1 0.9 fusion.65
  193.2 1.2 fusion.46
  194.5 95.4 %all-reduce.5.cloned.1.call-done = (f32[128,512]{1,0:T(8,128)}, f32[512,2048]{1,0:T(8,128)}, f32[512,512]{1,0:T(8,128)}) async-done(((f32[128,512]{1,0:T(8,128)}, f32[512,2048]{1,0:T(8,128)}, f32[512,512]{1,0:T(8,128)}), (f32[128,512]{1,0:T(8,128)}, f32[512,2048]{1,0:T(8,128)}, f32[512,512]{1,0:T(8,128)})) %all-reduce.5.cloned.1.call-update) | async-done | bytes 5505040 | tf_op jit(solution)/shard_map/psum | solution.py:262
  290.3 1.0 scatter_custom_fusion.3
  292.1 4.8 all-to-all-start.4
  296.9 1.4 scatter_custom_fusion.1
  298.3 1.1 reshape.390
  299.3 13.7 %all-to-all-done.4 = f32[32,10,128]{2,1,0:T(8,128)} async-done(((f32[32,10,128]{2,1,0:T(8,128)}), f32[32,10,128]{2,1,0:T(8,128)}, u32[]{:S(2)}, u32[]{:S(2)}) %all-to-all-start.4) | async-done | bytes 163872 | tf_op jit(solution)/shard_map/all_to_all | solution.py:287
  313.1 7.0 %all-to-all-start.3 = ((f32[32,10,512]{2,1,0:T(8,128)}), f32[32,10,512]{2,1,0:T(8,128)S(1)}, u32[]{:S(2)}, u32[]{:S(2)}) async-start(f32[32,10,512]{2,1,0:T(8,128)} %reshape.390), calls=%async_computation.3 | async-start | bytes 2097152 | tf_op jit(solution)/shard_map/all_to_all | solution.py:286
  321.4 1.9 fusion.28
  323.4 1.0 reshape.462
  324.4 2.6 scatter_custom_fusion.4
  327.0 45.8 %all-to-all-done.3 = f32[32,10,512]{2,1,0:T(8,128)S(1)} async-done(((f32[32,10,512]{2,1,0:T(8,128)}), f32[32,10,512]{2,1,0:T(8,128)S(1)}, u32[]{:S(2)}, u32[]{:S(2)}) %all-to-all-start.3) | async-done | bytes 655392 | tf_op jit(solution)/shard_map/all_to_all | solution.py:286
  372.8 0.9 reshape.446
  373.7 4.0 scatter_custom_fusion.2
  377.8 139.6 %all-reduce.7.cloned.1.call-done = (f32[128,512]{1,0:T(8,128)}, f32[512,2048]{1,0:T(8,128)}, f32[512,512]{1,0:T(8,128)}) async-done(((f32[128,512]{1,0:T(8,128)}, f32[512,2048]{1,0:T(8,128)}, f32[512,512]{1,0:T(8,128)}), (f32[128,512]{1,0:T(8,128)}, f32[512,2048]{1,0:T(8,128)}, f32[512,512]{1,0:T(8,128)})) %all-reduce.7.cloned.1.call-update) | async-done | bytes 5505040 | tf_op jit(solution)/shard_map/psum | solution.py:261
  517.3 4.9 broadcast_multiply_fusion
  522.2 1.1 broadcast_multiply_fusion.1
  (106 shorter events, 15.6 us)
Async XLA Ops:
  7.2 52.9 %copy-start = (bf16[512,2048]{1,0:T(8,128)(2,1)S(1)}, bf16[512,2048]{1,0:T(8,128)(2,1)}, u32[]{:S(2)}) copy-start(bf16[512,2048]{1,0:T(8,128)(2,1)} %param.19) | copy-start | bytes 6291460
  7.2 25.1 %copy-start.1 = (bf16[512,512]{1,0:T(8,128)(2,1)S(1)}, bf16[512,512]{1,0:T(8,128)(2,1)}, u32[]{:S(2)}) copy-start(bf16[512,512]{1,0:T(8,128)(2,1)} %param.16) | copy-start | bytes 1572868
  8.9 34.2 %copy-start.21 = (s32[128]{0:T(128)}, s32[128]{0:T(128)S(1)}, u32[]{:S(2)}) copy-start(s32[128]{0:T(128)S(1)} %fusion.57) | copy-start | bytes 1540
  10.7 14.4 %all-to-all-start = ((s32[32,1,10]{2,1,0:T(1,128)}), s32[32,1,10]{2,1,0:T(1,128)S(1)}, u32[]{:S(2)}, u32[]{:S(2)}) async-start(s32[32,1,10]{2,1,0:T(1,128)} %bitcast.9), calls=%async_computation | async-start | bytes 32768 | tf_op jit(solution)/shard_map/all_to_all | solution.py:92
  28.8 14.3 %copy-start.22 = (s32[128]{0:T(128)S(1)}, s32[128]{0:T(128)}, u32[]{:S(2)}) copy-start(s32[128]{0:T(128)} %param.15) | copy-start | bytes 1540
  29.6 10.8 %all-to-all-start.2 = ((bf16[32,10,128]{2,1,0:T(8,128)(2,1)}), bf16[32,10,128]{2,1,0:T(8,128)(2,1)S(1)}, u32[]{:S(2)}, u32[]{:S(2)}) async-start(bf16[32,10,128]{2,1,0:T(8,128)(2,1)} %broadcast_select_fusion.1), calls=%async_computation.2 | async-start | bytes 262144 | tf_op jit(solution)/shard_map/all_to_all | solution.py:106
  32.3 27.3 %copy-start.8 = (bf16[128,512]{1,0:T(8,128)(2,1)S(1)}, bf16[128,512]{1,0:T(8,128)(2,1)}, u32[]{:S(2)}) copy-start(bf16[128,512]{1,0:T(8,128)(2,1)} %param.18) | copy-start | bytes 393220
  40.4 18.2 %all-to-all-start.1 = ((bf16[32,10,512]{2,1,0:T(8,128)(2,1)}), bf16[32,10,512]{2,1,0:T(8,128)(2,1)S(1)}, u32[]{:S(2)}, u32[]{:S(2)}) async-start(bf16[32,10,512]{2,1,0:T(8,128)(2,1)} %broadcast_select_fusion), calls=%async_computation.1 | async-start | bytes 1048576 | tf_op jit(solution)/shard_map/all_to_all | solution.py:105
  43.0 41.9 %all-gather.5.cloned.1.call-start = ((), (), s32[]{:S(2)}) async-start(), calls=%async_computation.5 | async-start | bytes 1179648 | tf_op jit(solution)/shard_map/all_gather | solution.py:126
  43.7 16.2 %copy-start.18 = (pred[128]{0:T(512)(128)(4,1)}, pred[128]{0:T(512)(128)(4,1)S(1)}, u32[]{:S(2)}) copy-start(pred[128]{0:T(512)(128)(4,1)S(1)} %get-tuple-element.320) | copy-start | bytes 388
  44.4 17.2 %copy-start.10 = (bf16[128,128]{1,0:T(8,128)(2,1)}, bf16[128,128]{1,0:T(8,128)(2,1)S(1)}, u32[]{:S(2)}) copy-start(bf16[128,128]{1,0:T(8,128)(2,1)S(1)} %gather_fusion.3) | copy-start | bytes 98308
  59.9 27.3 %copy-start.14 = (f32[128]{0:T(128)}, f32[128]{0:T(128)S(1)}, u32[]{:S(2)}) copy-start(f32[128]{0:T(128)S(1)} %broadcast_multiply_fusion.8) | copy-start | bytes 1540
  60.1 27.1 %copy-start.16 = (f32[128]{0:T(128)}, f32[128]{0:T(128)S(1)}, u32[]{:S(2)}) copy-start(f32[128]{0:T(128)S(1)} %add_rsqrt_fusion.1) | copy-start | bytes 1540
  61.6 0.8 copy-start.7
  63.1 3.4 copy-start.4
  63.2 47.7 %all-gather.7.cloned.1.call-start = ((), (), s32[]{:S(2)}) async-start(), calls=%async_computation.6 | async-start | bytes 1179648 | tf_op jit(solution)/shard_map/all_gather | solution.py:127
  63.9 76.3 %all-gather.11.cloned.1.call-start = ((), (), s32[]{:S(2)}) async-start(), calls=%async_computation.8 | async-start | bytes 1179648 | tf_op jit(solution)/shard_map/all_gather | solution.py:208
  66.6 94.7 %all-gather.9.cloned.1.call-start = ((), (), s32[]{:S(2)}) async-start(), calls=%async_computation.7 | async-start | bytes 1179648 | tf_op jit(solution)/shard_map/all_gather | solution.py:209
  125.7 164.3 %all-reduce.5.cloned.1.call-start = ((), (), s32[]{:S(2)}) async-start(), calls=%async_computation.9 | async-start | bytes 11010048 | tf_op jit(solution)/shard_map/psum | solution.py:262
  164.1 9.2 %copy-start.3 = (bf16[128,512]{1,0:T(8,128)(2,1)S(1)}, bf16[128,512]{1,0:T(8,128)(2,1)}, u32[]{:S(2)}) copy-start(bf16[128,512]{1,0:T(8,128)(2,1)} %get-tuple-element.255) | copy-start | bytes 393220 | tf_op jit(solution)/shard_map/while/body/eval_jaxpr/cond
  174.1 5.9 %copy-start.13 = (pred[1024,128]{1,0:T(8,128)(4,1)S(1)}, pred[1024,128]{1,0:T(8,128)(4,1)}, u32[]{:S(2)}) copy-start(pred[1024,128]{1,0:T(8,128)(4,1)} %broadcast_compare_fusion) | copy-start | bytes 393220 | tf_op jit(solution)/shard_map/while/body/eval_jaxpr/cond
  185.7 6.5 %copy-start.15 = (f32[128]{0:T(128)S(1)}, f32[128]{0:T(128)}, u32[]{:S(2)}) copy-start(f32[128]{0:T(128)} %copy-done.14) | copy-start | bytes 1540
  185.7 6.4 %copy-start.17 = (f32[128]{0:T(128)S(1)}, f32[128]{0:T(128)}, u32[]{:S(2)}) copy-start(f32[128]{0:T(128)} %copy-done.16) | copy-start | bytes 1540
  188.5 4.5 copy-start.2
  188.5 4.7 copy-start.11
  188.5 4.7 copy-start.20
  194.4 95.5 %copy-start.9 = (bf16[128,512]{1,0:T(8,128)(2,1)S(1)}, bf16[128,512]{1,0:T(8,128)(2,1)}, u32[]{:S(2)}) copy-start(bf16[128,512]{1,0:T(8,128)(2,1)} %param.18) | copy-start | bytes 393220
  194.5 102.4 %copy-start.19 = (pred[128]{0:T(512)(128)(4,1)S(1)}, pred[128]{0:T(512)(128)(4,1)}, u32[]{:S(2)}) copy-start(pred[128]{0:T(512)(128)(4,1)} %copy-done.18) | copy-start | bytes 388
  194.5 322.8 %all-reduce.7.cloned.1.call-start = ((), (), s32[]{:S(2)}) async-start(), calls=%async_computation.10 | async-start | bytes 11010048 | tf_op jit(solution)/shard_map/psum | solution.py:261
  290.0 31.4 %copy-start.5 = (bf16[128,512]{1,0:T(8,128)(2,1)S(1)}, bf16[128,512]{1,0:T(8,128)(2,1)}, u32[]{:S(2)}) copy-start(bf16[128,512]{1,0:T(8,128)(2,1)} %get-tuple-element.310) | copy-start | bytes 393220
  292.1 21.0 %all-to-all-start.4 = ((f32[32,10,128]{2,1,0:T(8,128)}), f32[32,10,128]{2,1,0:T(8,128)}, u32[]{:S(2)}, u32[]{:S(2)}) async-start(f32[32,10,128]{2,1,0:T(8,128)} %reshape.392), calls=%async_computation.4 | async-start | bytes 524288 | tf_op jit(solution)/shard_map/all_to_all | solution.py:287
  313.1 59.7 %all-to-all-start.3 = ((f32[32,10,512]{2,1,0:T(8,128)}), f32[32,10,512]{2,1,0:T(8,128)S(1)}, u32[]{:S(2)}, u32[]{:S(2)}) async-start(f32[32,10,512]{2,1,0:T(8,128)} %reshape.390), calls=%async_computation.3 | async-start | bytes 2097152 | tf_op jit(solution)/shard_map/all_to_all | solution.py:286
  517.3 4.9 copy-start.6
  517.3 6.0 %copy-start.12 = (f32[128,512]{1,0:T(8,128)S(1)}, f32[128,512]{1,0:T(8,128)}, u32[]{:S(2)}) copy-start(f32[128,512]{1,0:T(8,128)} %get-tuple-element.306) | copy-start | bytes 786436
Sparse Core Ops, SparseCore 0:
  63.3 21.6 all-gather.4
  87.4 23.3 all-gather.6
  112.7 23.3 all-gather.10
  137.9 23.3 all-gather.8
  194.6 95.3 all-reduce.4
  292.4 224.8 all-reduce.6
